TPU v7x, 32 devices: a whole 2x2x4 slice. The times are simulated.
32 devices in a mesh: vir: 8 (over y, x, core), occ: 4 (over z).
Axes of the slice: x: 2, y: 2, z: 4, core: 2. Of those that a mesh axis runs over, the one named last changes fastest.
Arguments:
- perturbation: float32 [10240, 1024], P('vir', 'occ'), may hold values from -6 to 6
- eig_virtual: float32 [10240, 10240], P('vir', 'occ'), may hold values from -0.0625 to 0.0625
- eig_occupied: float32 [1024, 1024], P('occ'), may hold values from -0.1875 to 0.1875
- energy_virtual: float32 [10240], P('occ'), may hold values from 0.5 to 4
- energy_occupied: float32 [1024], replicated, may hold values from -4 to -0.5
Outputs:
- response: float32 [10240, 1024], P('vir', 'occ')
All inputs are finite; a program needn't handle non-finite values.
Results may differ from a plain program's by a relative error of at most 0.000078.
Values sent between devices are 32-bit elements; how exact they have to be, the bound alone decides.
No kernel may reach another device: no remote copies, remote signals or barrier semaphores. Data moves between devices by JAX's collectives and lax.ppermute only.
A program may use at most 128 MiB of HBM per device.

v0:
```python
import jax
import jax.numpy as jnp
from jax import lax
from jax.sharding import PartitionSpec as P


def body(perturbation, eig_virtual, eig_occupied, energy_virtual, energy_occupied):
    exact = lax.Precision.HIGHEST
    share = eig_virtual.shape[1] // lax.axis_size("vir")
    own_energy = lax.dynamic_slice_in_dim(energy_virtual, lax.axis_index("vir") * share, share, 0)
    denominator = own_energy[:, None] - energy_occupied[None, :]
    whole_rows = lax.all_gather(perturbation, "occ", axis=1, tiled=True)
    full_vectors = lax.all_gather(eig_occupied, "occ", axis=0, tiled=True)
    coarse = lax.psum_scatter(
        lax.dot_general(
            eig_virtual,
            whole_rows,
            (((0,), (0,)), ((), ())),
            precision=exact,
            preferred_element_type=jnp.float32,
        ),
        "vir",
        scatter_dimension=0,
        tiled=True,
    )
    projected = jnp.dot(coarse, full_vectors, precision=exact, preferred_element_type=jnp.float32)
    scaled = projected / denominator
    back_rows = lax.dot_general(
        scaled,
        full_vectors,
        (((1,), (1,)), ((), ())),
        precision=exact,
        preferred_element_type=jnp.float32,
    )
    gathered = lax.all_gather(back_rows, "vir", axis=0, tiled=True)
    spread = jnp.dot(eig_virtual, gathered, precision=exact, preferred_element_type=jnp.float32)
    return lax.psum_scatter(spread, "occ", scatter_dimension=1, tiled=True)


def solution(mesh):
    in_specs = (P("vir", "occ"), P("vir", "occ"), P("occ", None), P("occ"), P())
    out_specs = P("vir", "occ")
    return jax.shard_map(body, mesh=mesh, in_specs=in_specs, out_specs=out_specs, check_vma=False)
```

profile of v0, /device:TPU:0, one launch (start us, length us, event | category | flops | bytes accessed | tf_op | source)
XLA Modules:
  0.0 541.2 jit_solution(11509484725248971361)
XLA Ops:
  6.5 0.0 all-gather.4.cloned.1.call-start
  6.5 0.7 all-gather.4.cloned.1.call-update
  7.3 0.0 all-gather.6.cloned.1.call-start
  7.3 0.7 all-gather.6.cloned.1.call-update
  8.0 0.0 reduce-scatter.3.cloned.1.call-start
  8.1 101.6 %all-gather.4.cloned.1.call-done = f32[1280,1024]{1,0:T(8,128)} async-done(((f32[1280,256]{1,0:T(8,128)}), f32[1280,1024]{1,0:T(8,128)}) %all-gather.4.cloned.1.call-update) | async-done | bytes 5242896 | tf_op jit(solution)/shard_map/all_gather | solution.py:12
  109.7 47.1 %fusion = f32[2560,1024]{1,0:T(8,128)} fusion(f32[1280,2560]{1,0:T(8,128)} %param.6, f32[1280,1024]{1,0:T(8,128)} %all-gather.4.cloned.1.call-done), kind=kOutput, calls=%fused_computation.2 | convolution fusion | flops 40265318400 | bytes 28835840 | tf_op jit(solution)/shard_map/dot_general | solution.py:15
  156.8 0.0 copy-start.1
  156.8 0.0 reduce-scatter.3.cloned.1.call-update
  156.8 0.2 all-gather.8.cloned.1.call-start
  157.0 0.8 dynamic_slice.3
  157.8 32.6 %all-gather.6.cloned.1.call-done = f32[1024,1024]{1,0:T(8,128)} async-done(((f32[256,1024]{1,0:T(8,128)}), f32[1024,1024]{1,0:T(8,128)}) %all-gather.6.cloned.1.call-update) | async-done | bytes 4194320 | tf_op jit(solution)/shard_map/all_gather | solution.py:13
  190.4 84.0 %reduce-scatter.3.cloned.1.call-done = f32[320,1024]{1,0:T(8,128)} async-done(((f32[2560,1024]{1,0:T(8,128)}), f32[320,1024]{1,0:T(8,128)}) %reduce-scatter.3.cloned.1.call-update) | async-done | bytes 1310736 | tf_op jit(solution)/shard_map/reduce_scatter | solution.py:14
  274.4 0.0 copy-done.1
  274.4 0.0 copy-start
  274.4 7.2 %convolution_divide_fusion = f32[320,1024]{1,0:T(8,128)S(1)} fusion(f32[320,1024]{1,0:T(8,128)} %reduce-scatter.3.cloned.1.call-done, f32[1024,1024]{1,0:T(8,128)} %all-gather.6.cloned.1.call-done, f32[1024]{0:T(1024)S(1)} %copy-done.1, f32[320]{0:T(512)S(1)} %dynamic_slice.3), kind=kOutput, calls=%fused_computation.1 | convolution fusion | flops 4027187200 | bytes 6821120 | tf_op jit(solution)/shard_map/dot_general | solution.py:26
  281.6 0.0 copy-done
  281.6 5.5 %fusion.1 = f32[320,1024]{1,0:T(8,128)} fusion(f32[320,1024]{1,0:T(8,128)S(1)} %convolution_divide_fusion, f32[1024,1024]{1,0:T(8,128)S(1)} %copy-done), kind=kOutput, calls=%fused_computation.3 | convolution fusion | flops 4026531840 | bytes 6815744 | tf_op jit(solution)/shard_map/dot_general | solution.py:28
  287.1 0.0 all-gather.8.cloned.1.call-update
  287.1 0.0 reduce-scatter.5.cloned.1.call-start
  287.2 63.2 %all-gather.8.cloned.1.call-done = f32[2560,1024]{1,0:T(8,128)} async-done(((f32[320,1024]{1,0:T(8,128)}), f32[2560,1024]{1,0:T(8,128)}) %all-gather.8.cloned.1.call-update) | async-done | bytes 10485776 | tf_op jit(solution)/shard_map/all_gather | solution.py:35
  350.4 87.1 %convolution_bitcast_fusion = f32[1280,1024]{0,1:T(8,128)} fusion(f32[2560,1024]{1,0:T(8,128)} %all-gather.8.cloned.1.call-done, f32[1280,2560]{1,0:T(8,128)} %param.6), kind=kOutput, calls=%fused_computation | convolution fusion | flops 40265318400 | bytes 28835840 | tf_op jit(solution)/shard_map/dot_general | solution.py:36
  437.5 0.0 reduce-scatter.5.cloned.1.call-update
  437.5 93.9 %reduce-scatter.5.cloned.1.call-done = f32[1280,256]{0,1:T(8,128)} async-done(((f32[1280,1024]{0,1:T(8,128)}), f32[1280,256]{0,1:T(8,128)}) %reduce-scatter.5.cloned.1.call-update) | async-done | bytes 1310736 | tf_op jit(solution)/shard_map/reduce_scatter | solution.py:37
  531.5 2.8 copy.6
Async XLA Ops:
  6.5 103.2 %all-gather.4.cloned.1.call-start = ((), (), s32[]{:S(2)}) async-start(), calls=%async_computation.2 | async-start | bytes 6553600 | tf_op jit(solution)/shard_map/all_gather | solution.py:12
  7.3 183.1 %all-gather.6.cloned.1.call-start = ((), (), s32[]{:S(2)}) async-start(), calls=%async_computation.4 | async-start | bytes 5242880 | tf_op jit(solution)/shard_map/all_gather | solution.py:13
  8.0 266.4 %reduce-scatter.3.cloned.1.call-start = ((), (), s32[]{:S(2)}) async-start(), calls=%async_computation.3 | async-start | bytes 11796480 | tf_op jit(solution)/shard_map/reduce_scatter | solution.py:14
  156.8 117.6 %copy-start.1 = (f32[1024]{0:T(1024)S(1)}, f32[1024]{0:T(1024)}, u32[]{:S(2)}) copy-start(f32[1024]{0:T(1024)} %param.9) | copy-start | bytes 12292
  156.8 193.6 %all-gather.8.cloned.1.call-start = ((), (), s32[]{:S(2)}) async-start(), calls=%async_computation.5 | async-start | bytes 11796480 | tf_op jit(solution)/shard_map/all_gather | solution.py:35
  274.4 7.2 %copy-start = (f32[1024,1024]{1,0:T(8,128)S(1)}, f32[1024,1024]{1,0:T(8,128)}, u32[]{:S(2)}) copy-start(f32[1024,1024]{1,0:T(8,128)} %all-gather.6.cloned.1.call-done) | copy-start | bytes 12582916
  287.1 244.3 %reduce-scatter.5.cloned.1.call-start = ((), (), s32[]{:S(2)}) async-start(), calls=%async_computation.6 | async-start | bytes 6553600 | tf_op jit(solution)/shard_map/reduce_scatter | solution.py:37
Sparse Core Ops, SparseCore 0:
  8.9 100.7 all-gather.3
  111.3 79.0 all-gather.5
  193.9 80.4 reduce-scatter.2
  287.3 63.1 all-gather.7
  437.7 93.7 reduce-scatter.4
where the time goes:
time: 549 us; the launch traced here: 541 us
  waiting for transfers between devices  377 us (69%)
  matrix products  147 us (27%)
  between operations  13.5 us (2%)
    all_gather x1, waiting for transfers between devices, body(): whole_rows = lax.all_gather(perturbation, 'occ', axis=1, tiled=True)  102 us
    reduce_scatter x1, waiting for transfers between devices, body(): return lax.psum_scatter(spread, 'occ', scatter_dimension=1, tiled=True)  93.9 us
    dot_general x1, matrix products, body(): jnp.dot(eig_virtual, gathered, precision=exact, preferred_element_type=jn...  87.1 us
    reduce_scatter x1, waiting for transfers between devices, body(): lax.psum_scatter(lax.dot_general(eig_virtual, whole_rows, (((0,), (0,)),...  84 us
    all_gather x1, waiting for transfers between devices, body(): gathered = lax.all_gather(back_rows, 'vir', axis=0, tiled=True)  63.2 us
    dot_general x1, matrix products, body(): lax.dot_general(eig_virtual, whole_rows, (((0,), (0,)), ((), ())), precis...  47.1 us
    all_gather x1, waiting for transfers between devices, body(): full_vectors = lax.all_gather(eig_occupied, 'occ', axis=0, tiled=True)  32.6 us
  transfers between devices with their start and end apart: 5, of which 5 were waited for; matrix products, arithmetic and copies ran while one was open for 9% of the time, Pallas kernels for 0%

commit v1 on v0

--- a/solution.py
+++ b/solution.py
@@ -2,6 +2,35 @@
 import jax.numpy as jnp
 from jax import lax
 from jax.sharding import PartitionSpec as P
+
+
+def marks_track(vals):
+    carry = lax.psum(1, "occ")
+    n_now = lax.axis_index("occ")
+    w2, response, local_now = (carry, n_now, vals.shape[1])
+    all_rows = []
+    for to_i, d in enumerate(vals.shape):
+        all_rows.append(d * w2 if to_i == 1 else d)
+    finding = jnp.zeros(all_rows, vals.dtype)
+    k_now = lax.dynamic_update_slice_in_dim(finding, vals, response * local_now, axis=1)
+    piece_now = odd = vals
+    for s in range(1, w2 // 2 + 1):
+        pool = []
+        for to_i in range(w2):
+            pool.append((to_i, (to_i + 1) % w2))
+        piece_now = lax.ppermute(piece_now, "occ", pool)
+        k_now = lax.dynamic_update_slice_in_dim(
+            k_now, piece_now, (response - s) % w2 * local_now, axis=1
+        )
+        if 2 * s < w2:
+            all_blocks = []
+            for to_i in range(w2):
+                all_blocks.append((to_i, (to_i - 1) % w2))
+            odd = lax.ppermute(odd, "occ", all_blocks)
+            k_now = lax.dynamic_update_slice_in_dim(
+                k_now, odd, (response + s) % w2 * local_now, axis=1
+            )
+    return k_now
 
 
 def body(perturbation, eig_virtual, eig_occupied, energy_virtual, energy_occupied):
@@ -9,7 +38,7 @@
     share = eig_virtual.shape[1] // lax.axis_size("vir")
     own_energy = lax.dynamic_slice_in_dim(energy_virtual, lax.axis_index("vir") * share, share, 0)
     denominator = own_energy[:, None] - energy_occupied[None, :]
-    whole_rows = lax.all_gather(perturbation, "occ", axis=1, tiled=True)
+    whole_rows = marks_track(perturbation)
     full_vectors = lax.all_gather(eig_occupied, "occ", axis=0, tiled=True)
     coarse = lax.psum_scatter(
         lax.dot_general(

time: 549 us -> 584 us (1.064)
  starting transfers between devices: 0.33 us -> 45.1 us
  waiting for transfers between devices: 377 us -> 349 us
  local copies, waits for them, and re-layouts: 3.56 us -> 18.9 us
    ppermute x0 -> x3, waiting for transfers between devices: none -> 110 us  [the longest x2 77 us: marks_track(): piece_now = lax.ppermute(piece_now, 'occ', pool)]
    all_gather x1 -> x0, waiting for transfers between devices: 102 us -> none  [body(): whole_rows = lax.all_gather(perturbation, 'occ', axis=1, tiled=True)]
    reduce_scatter x1 -> x0, waiting for transfers between devices: 84 us -> none  [body(): lax.psum_scatter(lax.dot_general(eig_virtual, whole_rows, (((0,), (0,)),...]
    unnamed x5, waiting for transfers between devices: 1.46 us -> 81.2 us
    ppermute x0 -> x3, starting transfers between devices: none -> 45 us  [the longest x2 42.9 us: marks_track(): piece_now = lax.ppermute(piece_now, 'occ', pool)]
    all_gather x1, waiting for transfers between devices: 32.6 us -> 0.01 us  [body(): full_vectors = lax.all_gather(eig_occupied, 'occ', axis=0, tiled=True)]
    unnamed x4 -> x9, local copies, waits for them, and re-layouts: 0.01 us -> 11.4 us
  transfers between devices with their start and end apart: 5 -> 7, of which waited for: 5 -> 6; matrix products, arithmetic and copies ran while one was open for 9% -> 11% of each run, Pallas kernels for 0% -> 0%
where the time goes in v1:
time: 584 us; the launch traced here: 574 us
  waiting for transfers between devices  349 us (60%)
  matrix products  146 us (25%)
  starting transfers between devices  45.1 us (8%)
  local copies, waits for them, and re-layouts  18.9 us (3%)
  between operations  15.3 us (3%)
    reduce_scatter x1, waiting for transfers between devices, body(): return lax.psum_scatter(spread, 'occ', scatter_dimension=1, tiled=True)  93.9 us
    dot_general x1, matrix products, body(): jnp.dot(eig_virtual, gathered, precision=exact, preferred_element_type=jn...  87.1 us
    unnamed x5, waiting for transfers between devices  81.2 us
    ppermute x2, waiting for transfers between devices, marks_track(): piece_now = lax.ppermute(piece_now, 'occ', pool)  77 us
    all_gather x1, waiting for transfers between devices, body(): gathered = lax.all_gather(back_rows, 'vir', axis=0, tiled=True)  63.1 us
    dot_general x1, matrix products, body(): lax.dot_general(eig_virtual, whole_rows, (((0,), (0,)), ((), ())), precis...  46.5 us
    ppermute x2, starting transfers between devices, marks_track(): piece_now = lax.ppermute(piece_now, 'occ', pool)  42.9 us
    ppermute x1, waiting for transfers between devices, marks_track(): odd = lax.ppermute(odd, 'occ', all_blocks)  33.4 us
  transfers between devices with their start and end apart: 7, of which 6 were waited for; matrix products, arithmetic and copies ran while one was open for 11% of the time, Pallas kernels for 0%

profile of v1, /device:TPU:0, one launch (start us, length us, event | category | flops | bytes accessed | tf_op | source)
XLA Modules:
  0.0 574.3 jit_solution(6018823540006822388)
XLA Ops:
  7.4 0.0 all-gather.3.cloned.1.call-start
  7.4 0.7 all-gather.3.cloned.1.call-update
  8.1 0.0 reduce-scatter.7.cloned.1.call-start
  8.1 3.1 collective-permute-start
  11.2 2.1 collective-permute-start.1
  13.3 47.6 %collective-permute-done = f32[1280,256]{1,0:T(8,128)S(1)} collective-permute-done((f32[1280,256]{1,0:T(8,128)}, f32[1280,256]{1,0:T(8,128)S(1)}, u32[]{:S(2)}, u32[]{:S(2)}) %collective-permute-start) | collective-permute-done | bytes 1310752 | tf_op jit(solution)/shard_map/ppermute | solution.py:21
  61.0 39.8 %collective-permute-start.2 = (f32[1280,256]{1,0:T(8,128)S(1)}, f32[1280,256]{1,0:T(8,128)}, u32[]{:S(2)}, u32[]{:S(2)}) collective-permute-start(f32[1280,256]{1,0:T(8,128)S(1)} %collective-permute-done), channel_id=1, source_target_pairs={{0,1},{1,2},{2,3},{3,0},{4,5},{5,6},{6,7},{7,4},{8,9},{9,10},{10,1... | collective-permute-start | bytes 3932168 | tf_op jit(solution)/shard_map/ppermute | solution.py:21
  100.8 0.6 broadcast_in_dim.2
  101.4 0.0 copy-done.1
  101.4 0.2 constant_dynamic-update-slice_fusion.3
  101.6 0.2 constant_dynamic-update-slice_fusion.2
  101.8 33.4 %collective-permute-done.1 = f32[1280,256]{1,0:T(8,128)} collective-permute-done((f32[1280,256]{1,0:T(8,128)}, f32[1280,256]{1,0:T(8,128)}, u32[]{:S(2)}, u32[]{:S(2)}) %collective-permute-start.1) | collective-permute-done | bytes 1310752 | tf_op jit(solution)/shard_map/ppermute | solution.py:29
  135.2 1.5 constant_dynamic-update-slice_fusion.1
  136.7 29.3 %collective-permute-done.2 = f32[1280,256]{1,0:T(8,128)} collective-permute-done((f32[1280,256]{1,0:T(8,128)S(1)}, f32[1280,256]{1,0:T(8,128)}, u32[]{:S(2)}, u32[]{:S(2)}) %collective-permute-start.2) | collective-permute-done | bytes 1310752 | tf_op jit(solution)/shard_map/ppermute | solution.py:21
  166.0 1.5 constant_dynamic-update-slice_fusion
  167.5 0.0 copy-done.2
  167.5 46.5 %convolution_bitcast_fusion = f32[2560,1024]{0,1:T(8,128)} fusion(f32[1280,1024]{1,0:T(8,128)S(1)} %constant_dynamic-update-slice_fusion, f32[1280,2560]{1,0:T(8,128)S(1)} %copy-done.2), kind=kOutput, calls=%fused_computation | convolution fusion | flops 40265318400 | bytes 28835840 | tf_op jit(solution)/shard_map/dot_general | solution.py:44
  213.9 11.4 %copy.8 = f32[2560,1024]{1,0:T(8,128)} copy(f32[2560,1024]{0,1:T(8,128)} %convolution_bitcast_fusion) | data formatting | bytes 20971520
  225.3 0.0 reduce-scatter.7.cloned.1.call-update
  225.4 0.0 all-gather.5.cloned.1.call-start
  225.4 0.8 dynamic_slice.3
  226.2 80.4 %reduce-scatter.7.cloned.1.call-done = f32[320,1024]{1,0:T(8,128)} async-done(((f32[2560,1024]{1,0:T(8,128)}), f32[320,1024]{1,0:T(8,128)}) %reduce-scatter.7.cloned.1.call-update) | async-done | bytes 1310736
  306.6 7.3 %convolution_divide_fusion = f32[320,1024]{1,0:T(8,128)S(1)} fusion(f32[320,1024]{1,0:T(8,128)} %reduce-scatter.7.cloned.1.call-done, f32[1024,1024]{1,0:T(8,128)} %all-gather.3.cloned.1.call-done, f32[1024]{0:T(1024)S(1)} %copy-done.3, f32[320]{0:T(512)S(1)} %dynamic_slice.3), kind=kOutput, calls=%fused_computation.2 | convolution fusion | flops 4027187200 | bytes 6821120 | tf_op jit(solution)/shard_map/dot_general | solution.py:55
  314.0 0.0 copy-done
  314.0 5.5 fusion
  319.5 0.0 all-gather.5.cloned.1.call-update
  319.6 0.0 reduce-scatter.5.cloned.1.call-start
  319.6 63.1 %all-gather.5.cloned.1.call-done = f32[2560,1024]{1,0:T(8,128)} async-done(((f32[320,1024]{1,0:T(8,128)}), f32[2560,1024]{1,0:T(8,128)}) %all-gather.5.cloned.1.call-update) | async-done | bytes 10485776 | tf_op jit(solution)/shard_map/all_gather | solution.py:64
  382.7 87.1 %convolution_bitcast_fusion.1 = f32[1280,1024]{0,1:T(8,128)} fusion(f32[2560,1024]{1,0:T(8,128)} %all-gather.5.cloned.1.call-done, f32[1280,2560]{1,0:T(8,128)} %param.6), kind=kOutput, calls=%fused_computation.1 | convolution fusion | flops 40265318400 | bytes 28835840 | tf_op jit(solution)/shard_map/dot_general | solution.py:65
  469.8 0.0 reduce-scatter.5.cloned.1.call-update
  469.8 93.9 %reduce-scatter.5.cloned.1.call-done = f32[1280,256]{0,1:T(8,128)} async-done(((f32[1280,1024]{0,1:T(8,128)}), f32[1280,256]{0,1:T(8,128)}) %reduce-scatter.5.cloned.1.call-update) | async-done | bytes 1310736 | tf_op jit(solution)/shard_map/reduce_scatter | solution.py:66
  563.7 2.8 copy.7
  (6 shorter events, 0.0 us)
Async XLA Ops:
  7.4 94.0 %copy-start.1 = (f32[1280,256]{1,0:T(8,128)S(1)}, f32[1280,256]{1,0:T(8,128)}, u32[]{:S(2)}) copy-start(f32[1280,256]{1,0:T(8,128)} %param.5) | copy-start | bytes 3932164
  7.4 218.8 %all-gather.3.cloned.1.call-start = ((), (), s32[]{:S(2)}) async-start(), calls=%async_computation.2 | async-start | bytes 5242880 | tf_op jit(solution)/shard_map/all_gather | solution.py:42
  8.1 298.5 %reduce-scatter.7.cloned.1.call-start = ((), (), s32[]{:S(2)}) async-start(), calls=%async_computation.5 | async-start | bytes 11796480
  8.1 52.8 %collective-permute-start = (f32[1280,256]{1,0:T(8,128)}, f32[1280,256]{1,0:T(8,128)S(1)}, u32[]{:S(2)}, u32[]{:S(2)}) collective-permute-start(f32[1280,256]{1,0:T(8,128)} %param.5), channel_id=1, source_target_pairs={{0,1},{1,2},{2,3},{3,0},{4,5},{5,6},{6,7},{7,4},{8,9},{9,10},{10,1... | collective-permute-start | bytes 3932168 | tf_op jit(solution)/shard_map/ppermute | solution.py:21
  11.2 123.9 %collective-permute-start.1 = (f32[1280,256]{1,0:T(8,128)}, f32[1280,256]{1,0:T(8,128)}, u32[]{:S(2)}, u32[]{:S(2)}) collective-permute-start(f32[1280,256]{1,0:T(8,128)} %param.5), channel_id=1, source_target_pairs={{0,3},{1,0},{2,1},{3,2},{4,7},{5,4},{6,5},{7,6},{8,11},{9,8},{10,9... | collective-permute-start | bytes 3932168 | tf_op jit(solution)/shard_map/ppermute | solution.py:29
  61.0 105.0 %collective-permute-start.2 = (f32[1280,256]{1,0:T(8,128)S(1)}, f32[1280,256]{1,0:T(8,128)}, u32[]{:S(2)}, u32[]{:S(2)}) collective-permute-start(f32[1280,256]{1,0:T(8,128)S(1)} %collective-permute-done), channel_id=1, source_target_pairs={{0,1},{1,2},{2,3},{3,0},{4,5},{5,6},{6,7},{7,4},{8,9},{9,10},{10,1... | collective-permute-start | bytes 3932168 | tf_op jit(solution)/shard_map/ppermute | solution.py:21
  100.7 66.7 %copy-start.2 = (f32[1280,2560]{1,0:T(8,128)S(1)}, f32[1280,2560]{1,0:T(8,128)}, u32[]{:S(2)}) copy-start(f32[1280,2560]{1,0:T(8,128)} %param.6) | copy-start | bytes 39321604
  225.3 81.3 %copy-start.3 = (f32[1024]{0:T(1024)S(1)}, f32[1024]{0:T(1024)}, u32[]{:S(2)}) copy-start(f32[1024]{0:T(1024)} %param.9) | copy-start | bytes 12292
  225.4 157.3 %all-gather.5.cloned.1.call-start = ((), (), s32[]{:S(2)}) async-start(), calls=%async_computation.3 | async-start | bytes 11796480 | tf_op jit(solution)/shard_map/all_gather | solution.py:64
  306.6 7.4 %copy-start = (f32[1024,1024]{1,0:T(8,128)S(1)}, f32[1024,1024]{1,0:T(8,128)}, u32[]{:S(2)}) copy-start(f32[1024,1024]{1,0:T(8,128)} %all-gather.3.cloned.1.call-done) | copy-start | bytes 12582916
  319.6 244.2 %reduce-scatter.5.cloned.1.call-start = ((), (), s32[]{:S(2)}) async-start(), calls=%async_computation.4 | async-start | bytes 6553600 | tf_op jit(solution)/shard_map/reduce_scatter | solution.py:66
Sparse Core Ops, SparseCore 0:
  9.7 150.6 all-gather.2
  469.9 93.7 reduce-scatter.4
Sparse Core Ops, SparseCore 1:
  225.4 81.1 reduce-scatter.6
  319.6 63.0 all-gather.4
